TPU v7x, 256 devices: a whole 4x4x8 slice. The times are simulated.
256 devices in a mesh: row: 16 (over y, x), col: 2 (over core), ctx: 8 (over z).
Axes of the slice: x: 4, y: 4, z: 8, core: 2. Of those that a mesh axis runs over, the one named last changes fastest.
Arguments:
- queries: bfloat16 [8192, 6144], P(('col', 'ctx'), 'row'), may hold values from -16 to 16
- keys: bfloat16 [8192, 6144], P(('col', 'ctx'), 'row'), may hold values from -16 to 16
- values: bfloat16 [8192, 6144], P(('col', 'ctx'), 'row'), may hold values from -6 to 6
- out_weight: bfloat16 [6144, 6144], P('col', 'row'), may hold values from -0.078125 to 0.078125
- cotangent: bfloat16 [8192, 6144], P(('col', 'ctx'), 'row'), may hold values from -0.125 to 0.125
- block_mask: int32 [16, 16], replicated, may hold values from 0 to 1, as said below
Outputs:
- mixed_out: bfloat16 [8192, 6144], P(('col', 'ctx'), 'row')
- grad_weight: bfloat16 [6144, 6144], P(('col', 'ctx'), 'row')
Inputs may be any that keep to these rules, and one draw needn't show every extreme that they name: block_mask[i, i] is 1 for every block i, and block_mask[i, j] is 0 for j > i.
All inputs are finite; a program needn't handle non-finite values.
Results may differ from a plain program's by a relative error of at most 0.013.
Values may be sent and summed in bfloat16 or wider, within the bound.
A program may use at most 64 MiB of HBM per device.

v0:
```python
import math
import jax
import jax.numpy as jnp
from jax import lax
from jax.sharding import PartitionSpec as P

HD = 128
BLOCK = 512
NEGATIVE_FILL = -1e30


def attend_block(carried, query_heads, key_block, value_block, allowed, score_scale):
    run_max, run_sum, weighted = carried
    tok_rows, head_count, head_size = query_heads.shape
    key_heads = key_block.reshape(key_block.shape[0], head_count, head_size)
    value_heads = value_block.reshape(value_block.shape[0], head_count, head_size)
    scores = (
        jnp.einsum("thd,uhd->thu", query_heads, key_heads, preferred_element_type=jnp.float32)
        * score_scale
    )
    scores = jnp.where(allowed[:, None, None], scores, NEGATIVE_FILL)
    new_max = jnp.maximum(run_max, jnp.max(scores, axis=2))
    correction = jnp.exp(run_max - new_max)
    weights = jnp.where(allowed[:, None, None], jnp.exp(scores - new_max[:, :, None]), 0.0)
    new_sum = run_sum * correction + jnp.sum(weights, axis=2)
    product = jnp.einsum(
        "thu,uhd->thd",
        weights.astype(jnp.bfloat16),
        value_heads,
        preferred_element_type=jnp.float32,
    )
    new_weighted = weighted * correction[:, :, None] + product
    return (new_max, new_sum, new_weighted)


def body(queries, keys, values, out_weight, cotangent, block_mask):
    tok_rows, feature_width = queries.shape
    head_count = feature_width // HD
    query_heads = queries.reshape(tok_rows, head_count, HD)
    score_scale = 1.0 / math.sqrt(HD)
    local_blocks = tok_rows // BLOCK
    first_block = lax.axis_index(("col", "ctx")) * local_blocks
    local_mask = lax.dynamic_slice_in_dim(block_mask, first_block, local_blocks, 0)
    start_state = (
        jnp.full((tok_rows, head_count), NEGATIVE_FILL, jnp.float32),
        jnp.zeros((tok_rows, head_count), jnp.float32),
        jnp.zeros((tok_rows, head_count, HD), jnp.float32),
    )
    key_piece = lax.all_gather(keys, ("col", "ctx"), axis=0, tiled=True)
    value_piece = lax.all_gather(values, ("col", "ctx"), axis=0, tiled=True)
    block_count = key_piece.shape[0] // BLOCK
    key_stack = key_piece.reshape(block_count, BLOCK, feature_width)
    value_stack = value_piece.reshape(block_count, BLOCK, feature_width)
    block_columns = jnp.arange(block_count, dtype=jnp.int32)

    def one_block(state_in, entries):
        key_block, value_block, block_column = entries
        mask_column = lax.dynamic_index_in_dim(local_mask, block_column, 1, keepdims=False)
        allowed = jnp.repeat(mask_column, BLOCK, total_repeat_length=tok_rows) == 1
        updated = attend_block(state_in, query_heads, key_block, value_block, allowed, score_scale)
        return (updated, None)

    state_out, _ = lax.scan(one_block, start_state, (key_stack, value_stack, block_columns))
    run_max, run_sum, weighted = state_out
    attended = (
        (weighted / run_sum[:, :, None]).reshape(tok_rows, feature_width).astype(jnp.bfloat16)
    )
    all_heads = lax.all_gather(attended, "row", axis=1, tiled=True)
    head_columns = all_heads
    mixed_out = jnp.dot(
        head_columns,
        lax.all_gather(out_weight, "col", axis=0, tiled=True),
        preferred_element_type=jnp.float32,
    )
    head_columns = all_heads
    grad_weight = lax.psum_scatter(
        lax.dot_general(
            head_columns, cotangent, (((0,), (0,)), ((), ())), preferred_element_type=jnp.float32
        ),
        ("col", "ctx"),
        scatter_dimension=0,
        tiled=True,
    )
    return (mixed_out.astype(jnp.bfloat16), grad_weight.astype(jnp.bfloat16))


def solution(mesh):
    in_specs = (
        P(("col", "ctx"), "row"),
        P(("col", "ctx"), "row"),
        P(("col", "ctx"), "row"),
        P("col", "row"),
        P(("col", "ctx"), "row"),
        P(),
    )
    out_specs = (P(("col", "ctx"), "row"), P(("col", "ctx"), "row"))
    return jax.shard_map(body, mesh=mesh, in_specs=in_specs, out_specs=out_specs, check_vma=False)
```

profile of v0, /device:TPU:1, one launch (start us, length us, event | category | flops | bytes accessed | tf_op | source)
XLA Modules:
  0.0 622.6 jit_solution(9049366893125646251)
XLA Ops:
  12.0 48.1 %all-gather.5.cloned.1.call-done = bf16[8192,384]{1,0:T(8,128)(2,1)} async-done(((bf16[512,384]{1,0:T(8,128)(2,1)}), bf16[8192,384]{1,0:T(8,128)(2,1)}) %all-gather.5.cloned.1.call-update) | async-done | bytes 6291472 | tf_op jit(solution)/shard_map/all_gather | solution.py:49
  60.1 46.5 %all-gather.7.cloned.1.call-done = bf16[8192,384]{1,0:T(8,128)(2,1)} async-done(((bf16[512,384]{1,0:T(8,128)(2,1)}), bf16[8192,384]{1,0:T(8,128)(2,1)}) %all-gather.7.cloned.1.call-update) | async-done | bytes 6291472 | tf_op jit(solution)/shard_map/all_gather | solution.py:50
  107.2 304.6 %while.22 = (s32[]{:T(128)}, f32[512,3]{0,1:T(4,128)}, f32[512,3]{0,1:T(4,128)}, f32[512,3,128]{0,2,1:T(8,128)}, s32[16]{0:T(128)}, /*index=5*/s32[1,16]{1,0:T(1...) while((s32[]{:T(128)}, f32[512,3]{0,1:T(4,128)}, ...), condition=%wide.region_3.4_spmd.clone, body=%wide.region_0.3_spmd.clone.sunk | while | flops 413474304 | bytes 15433919 | solution.py:63
  111.5 1.9 constant_dynamic-slice_fusion.5
  114.3 2.4 bitcast_reduce_fusion.2
  118.7 1.9 copy.27
  120.7 3.4 fusion.42
  128.9 1.9 constant_dynamic-slice_fusion.5
  131.8 2.4 bitcast_reduce_fusion.2
  137.6 1.9 copy.27
  139.5 3.7 fusion.42
  148.1 1.9 constant_dynamic-slice_fusion.5
  151.0 2.4 bitcast_reduce_fusion.2
  156.8 1.9 copy.27
  158.7 3.7 fusion.42
  167.2 1.9 constant_dynamic-slice_fusion.5
  170.1 2.4 bitcast_reduce_fusion.2
  177.8 3.7 fusion.42
  186.4 1.9 constant_dynamic-slice_fusion.5
  189.2 2.4 bitcast_reduce_fusion.2
  197.0 3.7 fusion.42
  205.5 1.9 constant_dynamic-slice_fusion.5
  208.4 2.4 bitcast_reduce_fusion.2
  214.2 1.9 copy.27
  216.1 3.7 fusion.42
  224.6 1.9 constant_dynamic-slice_fusion.5
  227.5 2.4 bitcast_reduce_fusion.2
  235.2 3.7 fusion.42
  243.8 1.9 constant_dynamic-slice_fusion.5
  246.7 2.4 bitcast_reduce_fusion.2
  254.4 3.7 fusion.42
  262.9 1.9 constant_dynamic-slice_fusion.5
  265.8 2.4 bitcast_reduce_fusion.2
  273.5 3.7 fusion.42
  282.0 1.9 constant_dynamic-slice_fusion.5
  284.9 2.4 bitcast_reduce_fusion.2
  292.7 3.7 fusion.42
  301.2 1.9 constant_dynamic-slice_fusion.5
  304.1 2.4 bitcast_reduce_fusion.2
  311.8 3.7 fusion.42
  320.3 1.9 constant_dynamic-slice_fusion.5
  323.2 2.4 bitcast_reduce_fusion.2
  330.9 3.7 fusion.42
  339.5 1.9 constant_dynamic-slice_fusion.5
  342.4 2.4 bitcast_reduce_fusion.2
  348.1 1.9 copy.27
  350.1 3.7 fusion.42
  358.6 1.9 constant_dynamic-slice_fusion.5
  361.5 2.4 bitcast_reduce_fusion.2
  367.3 1.9 copy.27
  369.2 3.7 fusion.42
  377.7 1.9 constant_dynamic-slice_fusion.5
  380.6 2.4 bitcast_reduce_fusion.2
  388.3 3.7 fusion.42
  396.9 1.9 constant_dynamic-slice_fusion.5
  399.8 2.4 bitcast_reduce_fusion.2
  405.6 1.9 copy.27
  407.5 3.7 fusion.42
  411.7 2.0 divide_convert_fusion
  414.4 64.1 %all-gather.9.cloned.1.call-done = bf16[512,6144]{0,1:T(8,128)(2,1)} async-done(((bf16[512,384]{0,1:T(8,128)(2,1)}), bf16[512,6144]{0,1:T(8,128)(2,1)}) %all-gather.9.cloned.1.call-update) | async-done | bytes 6291472 | tf_op jit(solution)/shard_map/all_gather | solution.py:68
  478.5 9.9 %fusion.19 = f32[6144,384]{1,0:T(8,128)} fusion(bf16[512,6144]{0,1:T(8,128)(2,1)} %all-gather.9.cloned.1.call-done, bf16[512,384]{1,0:T(8,128)(2,1)S(1)} %copy-done), kind=kOutput, calls=%fused_computation.27 | convolution fusion | flops 2415919104 | bytes 16121856 | tf_op jit(solution)/shard_map/dot_general | solution.py:77
  488.4 12.0 %all-gather.11.cloned.1.call-done = bf16[6144,384]{1,0:T(8,128)(2,1)} async-done(((bf16[3072,384]{1,0:T(8,128)(2,1)}), bf16[6144,384]{1,0:T(8,128)(2,1)}) %all-gather.11.cloned.1.call-update) | async-done | bytes 4718608 | tf_op jit(solution)/shard_map/all_gather | solution.py:72
  500.4 8.3 %convolution_convert_fusion = bf16[512,384]{1,0:T(8,128)(2,1)} fusion(bf16[512,6144]{0,1:T(8,128)(2,1)} %all-gather.9.cloned.1.call-done, bf16[6144,384]{1,0:T(8,128)(2,1)} %all-gather.11.cloned.1.call-done), kind=kOutput, calls=%fused_computation.23 | convolution fusion | flops 2416115712 | bytes 11403264 | tf_op jit(solution)/shard_map/dot_general | solution.py:70
  508.7 105.5 %reduce-scatter.2.cloned.1.call-done = f32[384,384]{1,0:T(8,128)} async-done(((f32[6144,384]{1,0:T(8,128)}), f32[384,384]{1,0:T(8,128)}) %reduce-scatter.2.cloned.1.call-update) | async-done | bytes 589840 | tf_op jit(solution)/shard_map/reduce_scatter | solution.py:76
  (141 shorter events, 141.3 us)
Async XLA Ops:
  7.2 471.3 %copy-start = (bf16[512,384]{1,0:T(8,128)(2,1)S(1)}, bf16[512,384]{1,0:T(8,128)(2,1)}, u32[]{:S(2)}) copy-start(bf16[512,384]{1,0:T(8,128)(2,1)} %param.16) | copy-start | bytes 1179652
  7.2 53.0 %all-gather.5.cloned.1.call-start = ((), (), s32[]{:S(2)}) async-start(), calls=%async_computation.1 | async-start | bytes 6684672 | tf_op jit(solution)/shard_map/all_gather | solution.py:49
  7.9 98.7 %all-gather.7.cloned.1.call-start = ((), (), s32[]{:S(2)}) async-start(), calls=%async_computation.2 | async-start | bytes 6684672 | tf_op jit(solution)/shard_map/all_gather | solution.py:50
  8.7 469.8 %all-gather.9.cloned.1.call-start = ((), (), s32[]{:S(2)}) async-start(), calls=%async_computation.3 | async-start | bytes 6684672 | tf_op jit(solution)/shard_map/all_gather | solution.py:68
  413.7 86.7 %all-gather.11.cloned.1.call-start = ((), (), s32[]{:S(2)}) async-start(), calls=%async_computation.4 | async-start | bytes 7077888 | tf_op jit(solution)/shard_map/all_gather | solution.py:72
  414.3 200.0 %reduce-scatter.2.cloned.1.call-start = ((), (), s32[]{:S(2)}) async-start(), calls=%async_computation.5 | async-start | bytes 10027008 | tf_op jit(solution)/shard_map/reduce_scatter | solution.py:76
Sparse Core Ops, SparseCore 0:
  9.8 50.2 all-gather.4
  62.0 44.6 all-gather.6
  413.9 64.5 all-gather.8
  480.1 20.2 all-gather.10
  502.8 111.4 reduce-scatter.1
where the time goes:
time: 627 us; the launch traced here: 623 us
  waiting for transfers between devices  278 us (44%)
  matrix products  115 us (18%)
  local copies, waits for them, and re-layouts  110 us (18%)
  other arithmetic  75.8 us (12%)
  loops' own time  29.9 us (5%)
  between operations  13.8 us (2%)
    reduce_scatter x1, waiting for transfers between devices, body(): lax.psum_scatter(lax.dot_general(head_columns, cotangent, (((0,), (0,)),...  106 us
    dynamic_slice x64, local copies, waits for them, and re-layouts, body(): lax.scan(one_block, start_state, (key_stack, value_stack, block_columns))  96.5 us
    all_gather x1, waiting for transfers between devices, body(): all_heads = lax.all_gather(attended, 'row', axis=1, tiled=True)  64.1 us
    dot_general x16, matrix products, attend_block(): jnp.einsum('thu,uhd->thd', weights.astype(jnp.bfloat16), value_heads, pre...  58.4 us
    all_gather x1, waiting for transfers between devices, body(): key_piece = lax.all_gather(keys, ('col', 'ctx'), axis=0, tiled=True)  48.1 us
    all_gather x1, waiting for transfers between devices, body(): value_piece = lax.all_gather(values, ('col', 'ctx'), axis=0, tiled=True)  46.5 us
    dot_general x16, matrix products, attend_block(): jnp.einsum('thd,uhd->thu', query_heads, key_heads, preferred_element_type...  38.2 us
    another operation x1, loops' own time, body(): lax.scan(one_block, start_state, (key_stack, value_stack, block_columns))  29.9 us
  transfers between devices with their start and end apart: 5, of which 5 were waited for; matrix products, arithmetic and copies ran while one was open for 3% of the time, Pallas kernels for 0%

commit v1 on v0

--- a/solution.py
+++ b/solution.py
@@ -7,6 +7,16 @@
 HD = 128
 BLOCK = 512
 NEGATIVE_FILL = -1e30
+
+
+def gather_by_hops(x, mesh_axis, along):
+    count = lax.axis_size(mesh_axis)
+    current, blocks = (x, [x])
+    for _ in range(count - 1):
+        current = lax.ppermute(current, mesh_axis, [(i, (i + 1) % count) for i in range(count)])
+        blocks.insert(0, current)
+    line = jnp.concatenate(blocks, axis=along)
+    return jnp.roll(line, (lax.axis_index(mesh_axis) + 1) * x.shape[along], axis=along)
 
 
 def attend_block(carried, query_heads, key_block, value_block, allowed, score_scale):
@@ -65,7 +75,7 @@
     attended = (
         (weighted / run_sum[:, :, None]).reshape(tok_rows, feature_width).astype(jnp.bfloat16)
     )
-    all_heads = lax.all_gather(attended, "row", axis=1, tiled=True)
+    all_heads = gather_by_hops(attended, "row", 1)
     head_columns = all_heads
     mixed_out = jnp.dot(
         head_columns,

time: 627 us -> 752 us (1.20)
  waiting for transfers between devices: 278 us -> 383 us
  local copies, waits for them, and re-layouts: 110 us -> 132 us
    ppermute x0 -> x15, waiting for transfers between devices: none -> 176 us  [gather_by_hops(): lax.ppermute(current, mesh_axis, [(i, (i + 1) % count) for i in range(cou...]
    all_gather x1 -> x0, waiting for transfers between devices: 64.1 us -> none  [body(): all_heads = lax.all_gather(attended, 'row', axis=1, tiled=True)]
    unnamed x4 -> x61, local copies, waits for them, and re-layouts: 2.1 us -> 22.9 us
    all_gather x1, waiting for transfers between devices: 12 us -> 0.03 us  [body(): lax.all_gather(out_weight, 'col', axis=0, tiled=True)]
  transfers between devices with their start and end apart: 5 -> 19, of which waited for: 5 -> 18; matrix products, arithmetic and copies ran while one was open for 3% -> 4% of each run, Pallas kernels for 0% -> 0%
where the time goes in v1:
time: 752 us; the launch traced here: 747 us
  waiting for transfers between devices  383 us (51%)
  local copies, waits for them, and re-layouts  132 us (18%)
  matrix products  110 us (15%)
  other arithmetic  76 us (10%)
  loops' own time  29.4 us (4%)
  between operations  15.6 us (2%)
    ppermute x15, waiting for transfers between devices, gather_by_hops(): lax.ppermute(current, mesh_axis, [(i, (i + 1) % count) for i in range(cou...  176 us
    reduce_scatter x1, waiting for transfers between devices, body(): lax.psum_scatter(lax.dot_general(head_columns, cotangent, (((0,), (0,)),...  110 us
    dynamic_slice x64, local copies, waits for them, and re-layouts, body(): lax.scan(one_block, start_state, (key_stack, value_stack, block_columns))  97.5 us
    dot_general x16, matrix products, attend_block(): jnp.einsum('thu,uhd->thd', weights.astype(jnp.bfloat16), value_heads, pre...  57.7 us
    all_gather x1, waiting for transfers between devices, body(): key_piece = lax.all_gather(keys, ('col', 'ctx'), axis=0, tiled=True)  48 us
    all_gather x1, waiting for transfers between devices, body(): value_piece = lax.all_gather(values, ('col', 'ctx'), axis=0, tiled=True)  46.5 us
    dot_general x16, matrix products, attend_block(): jnp.einsum('thd,uhd->thu', query_heads, key_heads, preferred_element_type...  38.1 us
    another operation x1, loops' own time, body(): lax.scan(one_block, start_state, (key_stack, value_stack, block_columns))  29.4 us
  transfers between devices with their start and end apart: 19, of which 18 were waited for; matrix products, arithmetic and copies ran while one was open for 4% of the time, Pallas kernels for 0%

profile of v1, /device:TPU:1, one launch (start us, length us, event | category | flops | bytes accessed | tf_op | source)
XLA Modules:
  0.0 747.0 jit_solution(2190986435963714831)
XLA Ops:
  12.9 48.0 %all-gather.4.cloned.1.call-done = bf16[8192,384]{1,0:T(8,128)(2,1)} async-done(((bf16[512,384]{1,0:T(8,128)(2,1)}), bf16[8192,384]{1,0:T(8,128)(2,1)}) %all-gather.4.cloned.1.call-update) | async-done | bytes 6291472 | tf_op jit(solution)/shard_map/all_gather | solution.py:59
  61.0 46.5 %all-gather.6.cloned.1.call-done = bf16[8192,384]{1,0:T(8,128)(2,1)} async-done(((bf16[512,384]{1,0:T(8,128)(2,1)}), bf16[8192,384]{1,0:T(8,128)(2,1)}) %all-gather.6.cloned.1.call-update) | async-done | bytes 6291472 | tf_op jit(solution)/shard_map/all_gather | solution.py:60
  108.1 305.2 %while.22 = (s32[]{:T(128)}, f32[512,3]{0,1:T(4,128)}, f32[512,3]{0,1:T(4,128)}, f32[512,3,128]{0,2,1:T(8,128)}, s32[16]{0:T(128)}, /*index=5*/s32[1,16]{1,0:T(1...) while((s32[]{:T(128)}, f32[512,3]{0,1:T(4,128)}, ...), condition=%wide.region_3.4_spmd.clone, body=%wide.region_0.3_spmd.clone.sunk | while | flops 413474304 | bytes 15433919 | solution.py:73
  112.4 1.9 constant_dynamic-slice_fusion.5
  115.3 2.4 bitcast_reduce_fusion.2
  121.6 3.4 fusion.48
  130.0 1.9 constant_dynamic-slice_fusion.5
  132.9 2.4 bitcast_reduce_fusion.2
  140.5 3.6 fusion.48
  149.1 1.9 constant_dynamic-slice_fusion.5
  152.0 2.4 bitcast_reduce_fusion.2
  159.7 3.6 fusion.48
  168.3 1.9 constant_dynamic-slice_fusion.5
  171.2 2.4 bitcast_reduce_fusion.2
  178.9 3.6 fusion.48
  187.5 1.9 constant_dynamic-slice_fusion.5
  190.4 2.4 bitcast_reduce_fusion.2
  198.1 3.6 fusion.48
  206.7 1.9 constant_dynamic-slice_fusion.5
  209.6 2.4 bitcast_reduce_fusion.2
  217.3 3.6 fusion.48
  225.9 1.9 constant_dynamic-slice_fusion.5
  228.8 2.4 bitcast_reduce_fusion.2
  236.4 3.6 fusion.48
  245.0 1.9 constant_dynamic-slice_fusion.5
  247.9 2.4 bitcast_reduce_fusion.2
  255.6 3.6 fusion.48
  264.2 1.9 constant_dynamic-slice_fusion.5
  267.1 2.4 bitcast_reduce_fusion.2
  274.8 3.6 fusion.48
  283.4 1.9 constant_dynamic-slice_fusion.5
  286.3 2.4 bitcast_reduce_fusion.2
  294.0 3.6 fusion.48
  305.5 2.4 bitcast_reduce_fusion.2
  313.2 3.6 fusion.48
  324.6 2.4 bitcast_reduce_fusion.2
  332.3 3.6 fusion.48
  343.8 2.4 bitcast_reduce_fusion.2
  351.5 3.6 fusion.48
  363.0 2.4 bitcast_reduce_fusion.2
  370.7 3.6 fusion.48
  382.2 2.4 bitcast_reduce_fusion.2
  389.9 3.6 fusion.48
  401.4 2.4 bitcast_reduce_fusion.2
  409.1 3.6 fusion.48
  415.8 12.6 %collective-permute-done = bf16[512,384]{0,1:T(8,128)(2,1)S(1)} collective-permute-done((bf16[512,384]{0,1:T(8,128)(2,1)S(1)}, bf16[512,384]{0,1:T(8,128)(2,1)S(1)}, u32[]{:S(2)}, u32[]{:S(2)}) %collective-permute-start) | collective-permute-done | bytes 393248 | tf_op jit(solution)/shard_map/ppermute | solution.py:16
  428.3 12.8 %collective-permute-done.1 = bf16[512,384]{0,1:T(8,128)(2,1)S(1)} collective-permute-done((bf16[512,384]{0,1:T(8,128)(2,1)S(1)}, bf16[512,384]{0,1:T(8,128)(2,1)S(1)}, u32[]{:S(2)}, u32[]{:S(2)}) %collective-permute-start.1) | collective-permute-done | bytes 393248 | tf_op jit(solution)/shard_map/ppermute | solution.py:16
  441.2 11.9 %collective-permute-done.2 = bf16[512,384]{0,1:T(8,128)(2,1)S(1)} collective-permute-done((bf16[512,384]{0,1:T(8,128)(2,1)S(1)}, bf16[512,384]{0,1:T(8,128)(2,1)S(1)}, u32[]{:S(2)}, u32[]{:S(2)}) %collective-permute-start.2) | collective-permute-done | bytes 393248 | tf_op jit(solution)/shard_map/ppermute | solution.py:16
  453.1 11.0 %collective-permute-done.3 = bf16[512,384]{0,1:T(8,128)(2,1)S(1)} collective-permute-done((bf16[512,384]{0,1:T(8,128)(2,1)S(1)}, bf16[512,384]{0,1:T(8,128)(2,1)S(1)}, u32[]{:S(2)}, u32[]{:S(2)}) %collective-permute-start.3) | collective-permute-done | bytes 393248 | tf_op jit(solution)/shard_map/ppermute | solution.py:16
  464.1 9.9 %collective-permute-done.4 = bf16[512,384]{0,1:T(8,128)(2,1)S(1)} collective-permute-done((bf16[512,384]{0,1:T(8,128)(2,1)S(1)}, bf16[512,384]{0,1:T(8,128)(2,1)S(1)}, u32[]{:S(2)}, u32[]{:S(2)}) %collective-permute-start.4) | collective-permute-done | bytes 393248 | tf_op jit(solution)/shard_map/ppermute | solution.py:16
  474.1 9.9 %collective-permute-done.5 = bf16[512,384]{0,1:T(8,128)(2,1)S(1)} collective-permute-done((bf16[512,384]{0,1:T(8,128)(2,1)S(1)}, bf16[512,384]{0,1:T(8,128)(2,1)S(1)}, u32[]{:S(2)}, u32[]{:S(2)}) %collective-permute-start.5) | collective-permute-done | bytes 393248 | tf_op jit(solution)/shard_map/ppermute | solution.py:16
  484.0 9.9 %collective-permute-done.6 = bf16[512,384]{0,1:T(8,128)(2,1)S(1)} collective-permute-done((bf16[512,384]{0,1:T(8,128)(2,1)S(1)}, bf16[512,384]{0,1:T(8,128)(2,1)S(1)}, u32[]{:S(2)}, u32[]{:S(2)}) %collective-permute-start.6) | collective-permute-done | bytes 393248 | tf_op jit(solution)/shard_map/ppermute | solution.py:16
  494.0 10.8 %collective-permute-done.7 = bf16[512,384]{0,1:T(8,128)(2,1)S(1)} collective-permute-done((bf16[512,384]{0,1:T(8,128)(2,1)S(1)}, bf16[512,384]{0,1:T(8,128)(2,1)S(1)}, u32[]{:S(2)}, u32[]{:S(2)}) %collective-permute-start.7) | collective-permute-done | bytes 393248 | tf_op jit(solution)/shard_map/ppermute | solution.py:16
  505.5 11.2 %collective-permute-done.8 = bf16[512,384]{0,1:T(8,128)(2,1)S(1)} collective-permute-done((bf16[512,384]{0,1:T(8,128)(2,1)S(1)}, bf16[512,384]{0,1:T(8,128)(2,1)S(1)}, u32[]{:S(2)}, u32[]{:S(2)}) %collective-permute-start.8) | collective-permute-done | bytes 393248 | tf_op jit(solution)/shard_map/ppermute | solution.py:16
  517.4 12.2 %collective-permute-done.9 = bf16[512,384]{0,1:T(8,128)(2,1)S(1)} collective-permute-done((bf16[512,384]{0,1:T(8,128)(2,1)S(1)}, bf16[512,384]{0,1:T(8,128)(2,1)S(1)}, u32[]{:S(2)}, u32[]{:S(2)}) %collective-permute-start.9) | collective-permute-done | bytes 393248 | tf_op jit(solution)/shard_map/ppermute | solution.py:16
  530.4 13.3 %collective-permute-done.10 = bf16[512,384]{0,1:T(8,128)(2,1)S(1)} collective-permute-done((bf16[512,384]{0,1:T(8,128)(2,1)S(1)}, bf16[512,384]{0,1:T(8,128)(2,1)S(1)}, u32[]{:S(2)}, u32[]{:S(2)}) %collective-permute-start.10) | collective-permute-done | bytes 393248 | tf_op jit(solution)/shard_map/ppermute | solution.py:16
  544.5 14.1 %collective-permute-done.11 = bf16[512,384]{0,1:T(8,128)(2,1)S(1)} collective-permute-done((bf16[512,384]{0,1:T(8,128)(2,1)S(1)}, bf16[512,384]{0,1:T(8,128)(2,1)S(1)}, u32[]{:S(2)}, u32[]{:S(2)}) %collective-permute-start.11) | collective-permute-done | bytes 393248 | tf_op jit(solution)/shard_map/ppermute | solution.py:16
  559.3 13.2 %collective-permute-done.12 = bf16[512,384]{0,1:T(8,128)(2,1)S(1)} collective-permute-done((bf16[512,384]{0,1:T(8,128)(2,1)S(1)}, bf16[512,384]{0,1:T(8,128)(2,1)S(1)}, u32[]{:S(2)}, u32[]{:S(2)}) %collective-permute-start.12) | collective-permute-done | bytes 393248 | tf_op jit(solution)/shard_map/ppermute | solution.py:16
  573.3 12.3 %collective-permute-done.13 = bf16[512,384]{0,1:T(8,128)(2,1)} collective-permute-done((bf16[512,384]{0,1:T(8,128)(2,1)S(1)}, bf16[512,384]{0,1:T(8,128)(2,1)}, u32[]{:S(2)}, u32[]{:S(2)}) %collective-permute-start.13) | collective-permute-done | bytes 393248 | tf_op jit(solution)/shard_map/ppermute | solution.py:16
  585.8 11.0 %collective-permute-done.14 = bf16[512,384]{0,1:T(8,128)(2,1)} collective-permute-done((bf16[512,384]{0,1:T(8,128)(2,1)}, bf16[512,384]{0,1:T(8,128)(2,1)}, u32[]{:S(2)}, u32[]{:S(2)}) %collective-permute-start.14) | collective-permute-done | bytes 393248 | tf_op jit(solution)/shard_map/ppermute | solution.py:16
  607.9 5.5 copy-done.1
  613.4 5.8 fusion.18
  619.3 8.4 %fusion.22 = bf16[512,384]{1,0:T(8,128)(2,1)} fusion(bf16[6144,384]{1,0:T(8,128)(2,1)} %all-gather.8.cloned.1.call-done, bf16[512,12288]{0,1:T(8,128)(2,1)} %copy-done.1, s32[]{:T(128)S(6)} %select_n.86), kind=kOutput, calls=%fused_computation.27 | convolution fusion | flops 2416115712 | bytes 11403268 | tf_op jit(solution)/shard_map/dot_general | solution.py:80
  627.7 110.4 %reduce-scatter.2.cloned.1.call-done = f32[384,384]{1,0:T(8,128)} async-done(((f32[6144,384]{1,0:T(8,128)}), f32[384,384]{1,0:T(8,128)}) %reduce-scatter.2.cloned.1.call-update) | async-done | bytes 589840 | tf_op jit(solution)/shard_map/reduce_scatter | solution.py:86
  (226 shorter events, 185.8 us)
Async XLA Ops:
  8.0 605.4 %copy-start = (bf16[512,384]{1,0:T(8,128)(2,1)S(1)}, bf16[512,384]{1,0:T(8,128)(2,1)}, u32[]{:S(2)}) copy-start(bf16[512,384]{1,0:T(8,128)(2,1)} %param.16) | copy-start | bytes 1179652
  8.0 53.0 %all-gather.4.cloned.1.call-start = ((), (), s32[]{:S(2)}) async-start(), calls=%async_computation.1 | async-start | bytes 6684672 | tf_op jit(solution)/shard_map/all_gather | solution.py:59
  8.7 98.7 %all-gather.6.cloned.1.call-start = ((), (), s32[]{:S(2)}) async-start(), calls=%async_computation.2 | async-start | bytes 6684672 | tf_op jit(solution)/shard_map/all_gather | solution.py:60
  9.5 609.8 %all-gather.8.cloned.1.call-start = ((), (), s32[]{:S(2)}) async-start(), calls=%async_computation.3 | async-start | bytes 7077888 | tf_op jit(solution)/shard_map/all_gather | solution.py:82
  414.5 13.8 %collective-permute-start = (bf16[512,384]{0,1:T(8,128)(2,1)S(1)}, bf16[512,384]{0,1:T(8,128)(2,1)S(1)}, u32[]{:S(2)}, u32[]{:S(2)}) collective-permute-start(bf16[512,384]{0,1:T(8,128)(2,1)S(1)} %bitcast.57), channel_id=1, source_target_pairs={{0,16},{16,32},{32,48},{48,64},{64,80},{80,96},{96,112},{112,128},... | collective-permute-start | bytes 1179656 | tf_op jit(solution)/shard_map/ppermute | solution.py:16
  428.3 12.8 %collective-permute-start.1 = (bf16[512,384]{0,1:T(8,128)(2,1)S(1)}, bf16[512,384]{0,1:T(8,128)(2,1)S(1)}, u32[]{:S(2)}, u32[]{:S(2)}) collective-permute-start(bf16[512,384]{0,1:T(8,128)(2,1)S(1)} %collective-permute-done), channel_id=1, source_target_pairs={{0,16},{16,32},{32,48},{48,64},{64,80},{80,96},{96,112},{112,128},... | collective-permute-start | bytes 1179656 | tf_op jit(solution)/shard_map/ppermute | solution.py:16
  441.2 11.9 %collective-permute-start.2 = (bf16[512,384]{0,1:T(8,128)(2,1)S(1)}, bf16[512,384]{0,1:T(8,128)(2,1)S(1)}, u32[]{:S(2)}, u32[]{:S(2)}) collective-permute-start(bf16[512,384]{0,1:T(8,128)(2,1)S(1)} %collective-permute-done.1), channel_id=1, source_target_pairs={{0,16},{16,32},{32,48},{48,64},{64,80},{80,96},{96,112},{112,128},... | collective-permute-start | bytes 1179656 | tf_op jit(solution)/shard_map/ppermute | solution.py:16
  453.1 11.0 %collective-permute-start.3 = (bf16[512,384]{0,1:T(8,128)(2,1)S(1)}, bf16[512,384]{0,1:T(8,128)(2,1)S(1)}, u32[]{:S(2)}, u32[]{:S(2)}) collective-permute-start(bf16[512,384]{0,1:T(8,128)(2,1)S(1)} %collective-permute-done.2), channel_id=1, source_target_pairs={{0,16},{16,32},{32,48},{48,64},{64,80},{80,96},{96,112},{112,128},... | collective-permute-start | bytes 1179656 | tf_op jit(solution)/shard_map/ppermute | solution.py:16
  464.1 9.9 %collective-permute-start.4 = (bf16[512,384]{0,1:T(8,128)(2,1)S(1)}, bf16[512,384]{0,1:T(8,128)(2,1)S(1)}, u32[]{:S(2)}, u32[]{:S(2)}) collective-permute-start(bf16[512,384]{0,1:T(8,128)(2,1)S(1)} %collective-permute-done.3), channel_id=1, source_target_pairs={{0,16},{16,32},{32,48},{48,64},{64,80},{80,96},{96,112},{112,128},... | collective-permute-start | bytes 1179656 | tf_op jit(solution)/shard_map/ppermute | solution.py:16
  474.1 9.9 %collective-permute-start.5 = (bf16[512,384]{0,1:T(8,128)(2,1)S(1)}, bf16[512,384]{0,1:T(8,128)(2,1)S(1)}, u32[]{:S(2)}, u32[]{:S(2)}) collective-permute-start(bf16[512,384]{0,1:T(8,128)(2,1)S(1)} %collective-permute-done.4), channel_id=1, source_target_pairs={{0,16},{16,32},{32,48},{48,64},{64,80},{80,96},{96,112},{112,128},... | collective-permute-start | bytes 1179656 | tf_op jit(solution)/shard_map/ppermute | solution.py:16
  484.0 9.9 %collective-permute-start.6 = (bf16[512,384]{0,1:T(8,128)(2,1)S(1)}, bf16[512,384]{0,1:T(8,128)(2,1)S(1)}, u32[]{:S(2)}, u32[]{:S(2)}) collective-permute-start(bf16[512,384]{0,1:T(8,128)(2,1)S(1)} %collective-permute-done.5), channel_id=1, source_target_pairs={{0,16},{16,32},{32,48},{48,64},{64,80},{80,96},{96,112},{112,128},... | collective-permute-start | bytes 1179656 | tf_op jit(solution)/shard_map/ppermute | solution.py:16
  494.0 10.8 %collective-permute-start.7 = (bf16[512,384]{0,1:T(8,128)(2,1)S(1)}, bf16[512,384]{0,1:T(8,128)(2,1)S(1)}, u32[]{:S(2)}, u32[]{:S(2)}) collective-permute-start(bf16[512,384]{0,1:T(8,128)(2,1)S(1)} %collective-permute-done.6), channel_id=1, source_target_pairs={{0,16},{16,32},{32,48},{48,64},{64,80},{80,96},{96,112},{112,128},... | collective-permute-start | bytes 1179656 | tf_op jit(solution)/shard_map/ppermute | solution.py:16
  504.8 0.7 copy-start.2
  505.5 11.2 %collective-permute-start.8 = (bf16[512,384]{0,1:T(8,128)(2,1)S(1)}, bf16[512,384]{0,1:T(8,128)(2,1)S(1)}, u32[]{:S(2)}, u32[]{:S(2)}) collective-permute-start(bf16[512,384]{0,1:T(8,128)(2,1)S(1)} %collective-permute-done.7), channel_id=1, source_target_pairs={{0,16},{16,32},{32,48},{48,64},{64,80},{80,96},{96,112},{112,128},... | collective-permute-start | bytes 1179656 | tf_op jit(solution)/shard_map/ppermute | solution.py:16
  516.7 0.8 copy-start.4
  517.4 12.2 %collective-permute-start.9 = (bf16[512,384]{0,1:T(8,128)(2,1)S(1)}, bf16[512,384]{0,1:T(8,128)(2,1)S(1)}, u32[]{:S(2)}, u32[]{:S(2)}) collective-permute-start(bf16[512,384]{0,1:T(8,128)(2,1)S(1)} %collective-permute-done.8), channel_id=1, source_target_pairs={{0,16},{16,32},{32,48},{48,64},{64,80},{80,96},{96,112},{112,128},... | collective-permute-start | bytes 1179656 | tf_op jit(solution)/shard_map/ppermute | solution.py:16
  529.7 0.8 copy-start.6
  530.4 13.3 %collective-permute-start.10 = (bf16[512,384]{0,1:T(8,128)(2,1)S(1)}, bf16[512,384]{0,1:T(8,128)(2,1)S(1)}, u32[]{:S(2)}, u32[]{:S(2)}) collective-permute-start(bf16[512,384]{0,1:T(8,128)(2,1)S(1)} %collective-permute-done.9), channel_id=1, source_target_pairs={{0,16},{16,32},{32,48},{48,64},{64,80},{80,96},{96,112},{112,128},... | collective-permute-start | bytes 1179656 | tf_op jit(solution)/shard_map/ppermute | solution.py:16
  543.7 0.7 copy-start.8
  544.5 14.1 %collective-permute-start.11 = (bf16[512,384]{0,1:T(8,128)(2,1)S(1)}, bf16[512,384]{0,1:T(8,128)(2,1)S(1)}, u32[]{:S(2)}, u32[]{:S(2)}) collective-permute-start(bf16[512,384]{0,1:T(8,128)(2,1)S(1)} %collective-permute-done.10), channel_id=1, source_target_pairs={{0,16},{16,32},{32,48},{48,64},{64,80},{80,96},{96,112},{112,128},... | collective-permute-start | bytes 1179656 | tf_op jit(solution)/shard_map/ppermute | solution.py:16
  558.6 0.7 copy-start.10
  559.3 13.2 %collective-permute-start.12 = (bf16[512,384]{0,1:T(8,128)(2,1)S(1)}, bf16[512,384]{0,1:T(8,128)(2,1)S(1)}, u32[]{:S(2)}, u32[]{:S(2)}) collective-permute-start(bf16[512,384]{0,1:T(8,128)(2,1)S(1)} %collective-permute-done.11), channel_id=1, source_target_pairs={{0,16},{16,32},{32,48},{48,64},{64,80},{80,96},{96,112},{112,128},... | collective-permute-start | bytes 1179656 | tf_op jit(solution)/shard_map/ppermute | solution.py:16
  572.6 0.7 copy-start.12
  573.3 12.3 %collective-permute-start.13 = (bf16[512,384]{0,1:T(8,128)(2,1)S(1)}, bf16[512,384]{0,1:T(8,128)(2,1)}, u32[]{:S(2)}, u32[]{:S(2)}) collective-permute-start(bf16[512,384]{0,1:T(8,128)(2,1)S(1)} %collective-permute-done.12), channel_id=1, source_target_pairs={{0,16},{16,32},{32,48},{48,64},{64,80},{80,96},{96,112},{112,128},... | collective-permute-start | bytes 1179656 | tf_op jit(solution)/shard_map/ppermute | solution.py:16
  585.6 11.2 %collective-permute-start.14 = (bf16[512,384]{0,1:T(8,128)(2,1)}, bf16[512,384]{0,1:T(8,128)(2,1)}, u32[]{:S(2)}, u32[]{:S(2)}) collective-permute-start(bf16[512,384]{0,1:T(8,128)(2,1)} %collective-permute-done.13), channel_id=1, source_target_pairs={{0,16},{16,32},{32,48},{48,64},{64,80},{80,96},{96,112},{112,128},... | collective-permute-start | bytes 1179656 | tf_op jit(solution)/shard_map/ppermute | solution.py:16
  585.7 152.4 %reduce-scatter.2.cloned.1.call-start = ((), (), s32[]{:S(2)}) async-start(), calls=%async_computation.4 | async-start | bytes 10027008 | tf_op jit(solution)/shard_map/reduce_scatter | solution.py:86
  585.7 21.6 %copy-start.13 = (bf16[512,384]{0,1:T(8,128)(2,1)S(1)}, bf16[512,384]{0,1:T(8,128)(2,1)}, u32[]{:S(2)}) copy-start(bf16[512,384]{0,1:T(8,128)(2,1)} %copy-done.12) | copy-start | bytes 1179652
  585.7 21.7 %copy-start.11 = (bf16[512,384]{0,1:T(8,128)(2,1)S(1)}, bf16[512,384]{0,1:T(8,128)(2,1)}, u32[]{:S(2)}) copy-start(bf16[512,384]{0,1:T(8,128)(2,1)} %copy-done.10) | copy-start | bytes 1179652
  585.8 21.7 %copy-start.9 = (bf16[512,384]{0,1:T(8,128)(2,1)S(1)}, bf16[512,384]{0,1:T(8,128)(2,1)}, u32[]{:S(2)}) copy-start(bf16[512,384]{0,1:T(8,128)(2,1)} %copy-done.8) | copy-start | bytes 1179652
  585.8 21.7 %copy-start.7 = (bf16[512,384]{0,1:T(8,128)(2,1)S(1)}, bf16[512,384]{0,1:T(8,128)(2,1)}, u32[]{:S(2)}) copy-start(bf16[512,384]{0,1:T(8,128)(2,1)} %copy-done.6) | copy-start | bytes 1179652
  585.8 21.8 %copy-start.5 = (bf16[512,384]{0,1:T(8,128)(2,1)S(1)}, bf16[512,384]{0,1:T(8,128)(2,1)}, u32[]{:S(2)}) copy-start(bf16[512,384]{0,1:T(8,128)(2,1)} %copy-done.4) | copy-start | bytes 1179652
  585.8 21.8 %copy-start.3 = (bf16[512,384]{0,1:T(8,128)(2,1)S(1)}, bf16[512,384]{0,1:T(8,128)(2,1)}, u32[]{:S(2)}) copy-start(bf16[512,384]{0,1:T(8,128)(2,1)} %copy-done.2) | copy-start | bytes 1179652
  607.9 5.5 copy-start.1
Sparse Core Ops, SparseCore 0:
  10.7 50.2 all-gather.3
  62.8 44.6 all-gather.5
  619.4 118.6 reduce-scatter.1
Sparse Core Ops, SparseCore 1:
  585.7 33.4 all-gather.7
